TPU v7x, 256 devices: a whole 4x4x8 slice. The times are simulated.
256 devices in a mesh: dp: 32 (over z, y_lo, core), mp: 8 (over y_hi, x).
Axes of the slice: x: 4, y: 4 (y_hi: 2, y_lo: 2; y = y_hi * 2 + y_lo), z: 8, core: 2. Of those that a mesh axis runs over, the one named last changes fastest.
Arguments:
- upper_first: bfloat16 [8192, 4096], P('dp'), may hold values from -6 to 6
- upper_second: bfloat16 [8192, 4096], P('dp'), may hold values from -24 to 24
- grad_first: bfloat16 [8192, 4096], P('dp'), may hold values from -6 to 6
- grad_second: bfloat16 [8192, 4096], P('dp'), may hold values from -6 to 6
- norm_gain: bfloat16 [4096], replicated, may hold values from 0.25 to 1.75
- up_weight: bfloat16 [4096, 11264], P('dp', 'mp'), may hold values from -0.09375 to 0.09375
- down_weight: bfloat16 [4096, 11264], P('dp', 'mp'), may hold values from -0.0546875 to 0.0546875
- adapter_down: bfloat16 [4096, 64], replicated, may hold values from -0.09375 to 0.09375
- adapter_up: bfloat16 [64, 4096], replicated, may hold values from -0.75 to 0.75
Outputs:
- lower_first: bfloat16 [8192, 4096], P('dp', 'mp')
- lower_second: bfloat16 [8192, 4096], P('dp', 'mp')
- input_grad_first: bfloat16 [8192, 4096], P('dp', 'mp')
- input_grad_second: bfloat16 [8192, 4096], P('dp')
- adapter_down_grad: float32 [4096, 64], P('mp')
- adapter_up_grad: float32 [64, 4096], P(None, 'mp')
All inputs are finite; a program needn't handle non-finite values.
Results may differ from a plain program's by a relative error of at most 0.009.
Values may be sent and summed in bfloat16 or wider, within the bound.
A program may use at most 128 MiB of HBM per device.

v0:
```python
import math
import jax
import jax.numpy as jnp
from jax import lax
from jax.sharding import PartitionSpec as P

coupling = 0.5


def silu_slope(argument):
    sigmoid_value = jax.nn.sigmoid(argument)
    return sigmoid_value * (1.0 + argument * (1.0 - sigmoid_value))


def on_device(
    upper_first,
    upper_second,
    grad_first,
    grad_second,
    norm_gain,
    up_weight,
    down_weight,
    adapter_down,
    adapter_up,
):
    groups = lax.axis_size("mp")
    mp_rank = lax.axis_index("mp")
    model_width = upper_first.shape[1]
    share_width = model_width // groups
    offset = mp_rank * share_width
    tokens_all = upper_first.shape[0] * lax.axis_size("dp")
    grad_scale = 1.0 / math.sqrt(tokens_all)
    up_full = lax.all_gather(up_weight, "dp", axis=0, tiled=True)
    pre_adapter = jnp.dot(upper_first, adapter_down, preferred_element_type=jnp.float32)
    squashed = jax.nn.silu(pre_adapter).astype(jnp.bfloat16)
    adapted = jnp.dot(squashed, adapter_up, preferred_element_type=jnp.float32)
    lower_full = (upper_second.astype(jnp.float32) - adapted).astype(jnp.bfloat16)
    lower_value = lower_full.astype(jnp.float32)
    inverse_rms = lax.rsqrt(jnp.mean(lower_value * lower_value, axis=1, keepdims=True) + 1e-05)
    gain_full = norm_gain.astype(jnp.float32)
    normed = (lower_value * inverse_rms * gain_full).astype(jnp.bfloat16)
    hidden_pre = jnp.dot(normed, up_full, preferred_element_type=jnp.float32)
    activated = jax.nn.silu(hidden_pre).astype(jnp.bfloat16)
    down_full = lax.all_gather(down_weight, "dp", axis=0, tiled=True)
    partial_out = lax.dot_general(
        activated, down_full, (((1,), (1,)), ((), ())), preferred_element_type=jnp.float32
    )
    frozen_share = lax.psum_scatter(
        partial_out.astype(jnp.bfloat16), "mp", scatter_dimension=1, tiled=True
    ).astype(jnp.float32)
    upper_slice = lax.dynamic_slice_in_dim(upper_first, offset, share_width, 1)
    lower_first = ((upper_slice.astype(jnp.float32) - frozen_share) / coupling).astype(jnp.bfloat16)
    adapter_slope = jnp.einsum(
        "td,rd->tr", grad_second, adapter_up, preferred_element_type=jnp.float32
    )
    adapter_pre_grad = (adapter_slope * silu_slope(pre_adapter)).astype(jnp.bfloat16)
    back_adapter = jnp.einsum(
        "tr,dr->td", adapter_pre_grad, adapter_down, preferred_element_type=jnp.float32
    )
    carried = (grad_first.astype(jnp.float32) + back_adapter).astype(jnp.bfloat16)
    carried_slice = lax.dynamic_slice_in_dim(carried, offset, share_width, 1)
    input_grad_first = (coupling * carried_slice.astype(jnp.float32)).astype(jnp.bfloat16)
    down_grad_part = (
        jnp.einsum("td,tr->dr", upper_slice, adapter_pre_grad, preferred_element_type=jnp.float32)
        * grad_scale
    )
    second_slice = lax.dynamic_slice_in_dim(grad_second, offset, share_width, 1)
    up_grad_part = (
        jnp.einsum("tr,td->rd", squashed, second_slice, preferred_element_type=jnp.float32)
        * grad_scale
    )
    adapter_down_grad, adapter_up_grad = lax.psum((down_grad_part, up_grad_part), "dp")
    act_grad = jnp.dot(carried, down_full, preferred_element_type=jnp.float32)
    pre_grad = (act_grad * silu_slope(hidden_pre)).astype(jnp.bfloat16)
    normed_part = lax.dot_general(
        pre_grad, up_full, (((1,), (1,)), ((), ())), preferred_element_type=jnp.float32
    )
    stat_part = jnp.sum(hidden_pre * pre_grad.astype(jnp.float32), axis=1)
    normed_grad, curvature = lax.psum((normed_part, stat_part), "mp")
    correction = lower_value * inverse_rms * inverse_rms * curvature[:, None] / model_width
    input_grad_second = (
        grad_second.astype(jnp.float32) + inverse_rms * gain_full * normed_grad - correction
    ).astype(jnp.bfloat16)
    lower_second = lax.dynamic_slice_in_dim(lower_full, offset, share_width, 1)
    return (
        lower_first,
        lower_second,
        input_grad_first,
        input_grad_second,
        adapter_down_grad,
        adapter_up_grad,
    )


def solution(mesh):
    return jax.shard_map(
        on_device,
        mesh=mesh,
        in_specs=(
            P("dp", None),
            P("dp", None),
            P("dp", None),
            P("dp", None),
            P(),
            P("dp", "mp"),
            P("dp", "mp"),
            P(),
            P(),
        ),
        out_specs=(
            P("dp", "mp"),
            P("dp", "mp"),
            P("dp", "mp"),
            P("dp", None),
            P("mp", None),
            P(None, "mp"),
        ),
        check_vma=False,
    )
```

profile of v0, /device:TPU:1, one launch (start us, length us, event | category | flops | bytes accessed | tf_op | source)
XLA Modules:
  0.0 618.4 jit_solution(9565982590470995360)
XLA Ops:
  7.2 0.0 copy-start
  7.2 0.0 all-gather.3.cloned.1.call-start
  7.2 0.7 all-gather.3.cloned.1.call-update
  7.9 0.0 all-gather.5.cloned.1.call-start
  8.0 0.7 all-gather.5.cloned.1.call-update
  8.7 0.0 all-reduce.4.cloned.1.call-start
  8.7 0.0 copy-start.5
  8.7 0.8 convert_element_type.65
  9.6 2.4 fusion.22
  12.0 0.0 copy-done
  12.0 0.0 copy-done.5
  12.0 0.0 copy-start.1
  12.0 2.2 fusion.9
  14.3 0.0 copy-start.2
  14.3 0.0 copy-start.3
  14.3 0.0 copy-done.1
  14.3 0.8 fusion.15
  15.0 0.8 copy-done.2
  15.8 0.1 copy-done.3
  15.9 2.1 fusion.1
  18.0 72.4 %all-gather.3.cloned.1.call-done = bf16[4096,1408]{1,0:T(8,128)(2,1)} async-done(((bf16[128,1408]{1,0:T(8,128)(2,1)}), bf16[4096,1408]{1,0:T(8,128)(2,1)}) %all-gather.3.cloned.1.call-update) | async-done | bytes 11534352 | tf_op jit(solution)/shard_map/all_gather | solution.py:33
  90.4 9.6 %fusion.11 = f32[256,1408]{1,0:T(8,128)} fusion(bf16[4096,1408]{1,0:T(8,128)(2,1)} %all-gather.3.cloned.1.call-done, bf16[256,4096]{1,0:T(8,128)(2,1)} %get-tuple-element.9, f32[4096]{0:T(1024)S(1)} %convert_element_type.65, f32[256]{0:T(256)S(1)} %add_rsqrt_fusion), kind=kOutput, calls=%fused_computation.17 | convolution fusion | flops 2956984320 | bytes 15090688 | tf_op jit(solution)/shard_map/dot_general | solution.py:42
  99.9 67.4 %all-gather.5.cloned.1.call-done = bf16[4096,1408]{1,0:T(8,128)(2,1)} async-done(((bf16[128,1408]{1,0:T(8,128)(2,1)}), bf16[4096,1408]{1,0:T(8,128)(2,1)}) %all-gather.5.cloned.1.call-update) | async-done | bytes 11534352 | tf_op jit(solution)/shard_map/all_gather | solution.py:44
  167.3 0.0 copy-start.4
  167.3 9.0 %multiply_reduce_fusion = (f32[256]{0:T(256)S(1)}, bf16[256,1408]{1,0:T(8,128)(2,1)S(1)}) fusion(f32[256,1408]{1,0:T(8,128)} %fusion.11, bf16[256,4096]{1,0:T(8,128)(2,1)} %fusion.1, bf16[4096,1408]{1,0:T(8,128)(2,1)} %all-gather.5.cloned.1.call-done), kind=kOutput, calls=%fused_computation.20 | convolution fusion | flops 2957115136 | bytes 15795200 | tf_op jit(solution)/shard_map/dot_general | solution.py:73
  176.3 0.0 copy-done.4
  176.3 5.0 fusion.23
  181.3 0.0 all-reduce.4.cloned.1.call-update
  181.4 0.2 reduce-scatter.2.cloned.1.call-start
  181.6 9.6 %convolution_convert_fusion = bf16[256,4096]{1,0:T(8,128)(2,1)} fusion(bf16[4096,1408]{1,0:T(8,128)(2,1)} %all-gather.5.cloned.1.call-done, f32[256,1408]{1,0:T(8,128)} %fusion.11), kind=kOutput, calls=%fused_computation.6 | convolution fusion | flops 2955640832 | bytes 15073280 | tf_op jit(solution)/shard_map/dot_general | solution.py:45
  191.1 0.0 reduce-scatter.2.cloned.1.call-update
  191.2 0.0 all-reduce.6.cloned.1.call-start
  191.2 1.8 convolution_multiply_fusion.1
  193.0 0.8 convolution_multiply_fusion.2
  193.9 0.0 all-reduce.6.cloned.1.call-update
  193.9 1.7 constant_dynamic-slice_fusion
  195.6 1.7 multiply_convert_fusion.2
  197.2 21.3 %psum.29 = f32[256]{0:T(256)S(1)} all-reduce(f32[256]{0:T(256)S(1)} %get-tuple-element.10), channel_id=1, replica_groups=mesh['dp'=32,'mp'=8] {'mp'}, use_global_device_ids=true, to_apply=%region_4.5 | all-reduce | flops 256 | bytes 2048 | tf_op jit(solution)/shard_map/psum | solution.py:79
  218.5 76.4 %all-reduce.4.cloned.1.call-done = f32[256,4096]{1,0:T(8,128)} async-done(((f32[256,4096]{1,0:T(8,128)}), f32[256,4096]{1,0:T(8,128)}) %all-reduce.4.cloned.1.call-update) | async-done | bytes 4194320 | tf_op jit(solution)/shard_map/psum | solution.py:79
  294.9 5.8 fusion.8
  300.7 77.4 %reduce-scatter.2.cloned.1.call-done = bf16[256,512]{1,0:T(8,128)(2,1)} async-done(((bf16[256,4096]{1,0:T(8,128)(2,1)}), bf16[256,512]{1,0:T(8,128)(2,1)}) %reduce-scatter.2.cloned.1.call-update) | async-done | bytes 262160 | tf_op jit(solution)/shard_map/reduce_scatter | solution.py:48
  378.1 1.8 multiply_convert_fusion.3
  379.9 228.8 %all-reduce.6.cloned.1.call-done = (f32[512,64]{0,1:T(8,128)}, f32[64,512]{1,0:T(8,128)}) async-done(((f32[512,64]{0,1:T(8,128)}, f32[64,512]{1,0:T(8,128)}), (f32[512,64]{0,1:T(8,128)}, f32[64,512]{1,0:T(8,128)})) %all-reduce.6.cloned.1.call-update) | async-done | bytes 262160 | tf_op jit(solution)/shard_map/psum | solution.py:72
  608.8 1.6 copy.18
  610.4 1.6 copy.19
  (1 shorter events, 0.0 us)
Async XLA Ops:
  7.2 4.8 copy-start
  7.2 83.2 %all-gather.3.cloned.1.call-start = ((), (), s32[]{:S(2)}) async-start(), calls=%async_computation.1 | async-start | bytes 11894784 | tf_op jit(solution)/shard_map/all_gather | solution.py:33
  7.9 159.4 %all-gather.5.cloned.1.call-start = ((), (), s32[]{:S(2)}) async-start(), calls=%async_computation.2 | async-start | bytes 11894784 | tf_op jit(solution)/shard_map/all_gather | solution.py:44
  8.7 286.3 %all-reduce.4.cloned.1.call-start = ((), (), s32[]{:S(2)}) async-start(), calls=%async_computation.4 | async-start | bytes 8388608 | tf_op jit(solution)/shard_map/psum | solution.py:79
  8.7 3.3 copy-start.5
  12.0 2.2 copy-start.1
  14.3 1.6 copy-start.2
  14.3 1.7 copy-start.3
  167.3 9.0 %copy-start.4 = (bf16[4096,1408]{1,0:T(8,128)(2,1)S(1)}, bf16[4096,1408]{1,0:T(8,128)(2,1)}, u32[]{:S(2)}) copy-start(bf16[4096,1408]{1,0:T(8,128)(2,1)} %all-gather.3.cloned.1.call-done) | copy-start | bytes 34603012
  181.4 196.8 %reduce-scatter.2.cloned.1.call-start = ((), (), s32[]{:S(2)}) async-start(), calls=%async_computation.3 | async-start | bytes 2359296 | tf_op jit(solution)/shard_map/reduce_scatter | solution.py:48
  191.2 417.6 %all-reduce.6.cloned.1.call-start = ((), (), s32[]{:S(2)}) async-start(), calls=%async_computation.5 | async-start | bytes 524288 | tf_op jit(solution)/shard_map/psum | solution.py:72
Sparse Core Ops, SparseCore 0:
  9.8 80.4 all-gather.2
  92.2 75.0 all-gather.4
  181.5 113.4 all-reduce.3
  298.9 79.2 reduce-scatter.1
  381.2 227.5 all-reduce.5
where the time goes:
time: 619 us; the launch traced here: 618 us
  waiting for transfers between devices  524 us (85%)
  matrix products  43.3 us (7%)
  blocking collectives  21.3 us (3%)
  between operations  13.9 us (2%)
  other arithmetic  10.2 us (2%)
    psum x1, waiting for transfers between devices, on_device(): lax.psum((down_grad_part, up_grad_part), 'dp')  229 us
    reduce_scatter x1, waiting for transfers between devices, on_device(): lax.psum_scatter(partial_out.astype(jnp.bfloat16), 'mp', scatter_dimensio...  77.4 us
    psum x1, waiting for transfers between devices, on_device(): normed_grad, curvature = lax.psum((normed_part, stat_part), 'mp')  76.4 us
    all_gather x1, waiting for transfers between devices, on_device(): up_full = lax.all_gather(up_weight, 'dp', axis=0, tiled=True)  72.4 us
    all_gather x1, waiting for transfers between devices, on_device(): down_full = lax.all_gather(down_weight, 'dp', axis=0, tiled=True)  67.4 us
    psum x1, blocking collectives, on_device(): normed_grad, curvature = lax.psum((normed_part, stat_part), 'mp')  21.3 us
  transfers between devices with their start and end apart: 5, of which 5 were waited for; matrix products, arithmetic and copies ran while one was open for 7% of the time, Pallas kernels for 0%

commit v1 on v0

--- a/solution.py
+++ b/solution.py
@@ -41,7 +41,17 @@
     normed = (lower_value * inverse_rms * gain_full).astype(jnp.bfloat16)
     hidden_pre = jnp.dot(normed, up_full, preferred_element_type=jnp.float32)
     activated = jax.nn.silu(hidden_pre).astype(jnp.bfloat16)
-    down_full = lax.all_gather(down_weight, "dp", axis=0, tiled=True)
+
+    def plan_domain(body, shard_axis):
+        current_value = jnp.concatenate(
+            lax.all_to_all(
+                jnp.stack([body for _ in range(lax.axis_size(shard_axis))]), shard_axis, 0, 0
+            ),
+            axis=0,
+        )
+        return current_value
+
+    down_full = plan_domain(down_weight, "dp")
     partial_out = lax.dot_general(
         activated, down_full, (((1,), (1,)), ((), ())), preferred_element_type=jnp.float32
     )

time: 619 us -> 789 us (1.27)
  waiting for transfers between devices: 524 us -> 676 us
  starting transfers between devices: 0.38 us -> 11.8 us
    all_gather x1, waiting for transfers between devices: 72.4 us -> 220 us  [on_device(): up_full = lax.all_gather(up_weight, 'dp', axis=0, tiled=True)]
    all_to_all x0 -> x1, waiting for transfers between devices: none -> 68.7 us  [plan_domain(): lax.all_to_all(jnp.stack([body for _ in range(lax.axis_size(shard_axis))]...]
    all_gather x1 -> x0, waiting for transfers between devices: 67.4 us -> none  [on_device(): down_full = lax.all_gather(down_weight, 'dp', axis=0, tiled=True)]
    all_to_all x0 -> x1, starting transfers between devices: none -> 11.4 us  [plan_domain(): lax.all_to_all(jnp.stack([body for _ in range(lax.axis_size(shard_axis))]...]
  transfers between devices with their start and end apart: 5 -> 5, of which waited for: 5 -> 5; matrix products, arithmetic and copies ran while one was open for 7% -> 6% of each run, Pallas kernels for 0% -> 0%
where the time goes in v1:
time: 789 us; the launch traced here: 788 us
  waiting for transfers between devices  676 us (86%)
  matrix products  41.5 us (5%)
  blocking collectives  22.3 us (3%)
  between operations  13.9 us (2%)
  local copies, waits for them, and re-layouts  13.1 us (2%)
  starting transfers between devices  11.8 us (1%)
  other arithmetic  9.33 us (1%)
    psum x1, waiting for transfers between devices, on_device(): lax.psum((down_grad_part, up_grad_part), 'dp')  229 us
    all_gather x1, waiting for transfers between devices, on_device(): up_full = lax.all_gather(up_weight, 'dp', axis=0, tiled=True)  220 us
    psum x1, waiting for transfers between devices, on_device(): normed_grad, curvature = lax.psum((normed_part, stat_part), 'mp')  80.6 us
    reduce_scatter x1, waiting for transfers between devices, on_device(): lax.psum_scatter(partial_out.astype(jnp.bfloat16), 'mp', scatter_dimensio...  77.5 us
    all_to_all x1, waiting for transfers between devices, plan_domain(): lax.all_to_all(jnp.stack([body for _ in range(lax.axis_size(shard_axis))]...  68.7 us
    psum x1, blocking collectives, on_device(): normed_grad, curvature = lax.psum((normed_part, stat_part), 'mp')  22.3 us
  transfers between devices with their start and end apart: 5, of which 5 were waited for; matrix products, arithmetic and copies ran while one was open for 6% of the time, Pallas kernels for 0%

profile of v1, /device:TPU:1, one launch (start us, length us, event | category | flops | bytes accessed | tf_op | source)
XLA Modules:
  0.0 788.2 jit_solution(3163067554819196616)
XLA Ops:
  7.2 0.0 copy-start
  7.2 0.0 all-gather.2.cloned.1.call-start
  7.2 0.7 all-gather.2.cloned.1.call-update
  7.9 6.6 stack.2
  14.5 0.0 copy-start.5
  14.5 0.0 copy-start.2
  14.5 0.0 copy-start.4
  14.5 11.4 %all-to-all-start = ((bf16[32,128,1408]{2,1,0:T(8,128)(2,1)}), bf16[32,128,1408]{2,1,0:T(8,128)(2,1)}, u32[]{:S(2)}, u32[]{:S(2)}) async-start(bf16[32,128,1408]{2,1,0:T(8,128)(2,1)} %stack.2), calls=%async_computation | async-start | bytes 23068672 | tf_op jit(solution)/shard_map/all_to_all | solution.py:47
  26.0 0.0 all-reduce.4.cloned.1.call-start
  26.0 0.0 copy-done.5
  26.0 0.0 copy-start.7
  26.0 0.0 copy-done.2
  26.1 0.0 copy-done.4
  26.1 0.8 fusion.22
  26.8 0.0 copy-done
  26.8 0.8 copy-done.7
  27.6 0.0 copy-start.1
  27.6 2.2 fusion.9
  29.8 0.0 copy-start.3
  29.8 0.0 copy-done.1
  29.9 0.8 fusion.15
  30.6 0.9 copy-done.3
  31.5 2.1 fusion.1
  33.6 219.9 %all-gather.2.cloned.1.call-done = bf16[4096,1408]{1,0:T(8,128)(2,1)} async-done(((bf16[128,1408]{1,0:T(8,128)(2,1)}), bf16[4096,1408]{1,0:T(8,128)(2,1)}) %all-gather.2.cloned.1.call-update) | async-done | bytes 11534352 | tf_op jit(solution)/shard_map/all_gather | solution.py:33
  253.4 9.5 %fusion.11 = f32[256,1408]{1,0:T(8,128)} fusion(bf16[4096,1408]{1,0:T(8,128)(2,1)} %all-gather.2.cloned.1.call-done, bf16[256,4096]{1,0:T(8,128)(2,1)} %get-tuple-element.9, f32[4096]{0:T(1024)S(1)} %convert_element_type.65, f32[256]{0:T(256)S(1)} %add_rsqrt_fusion), kind=kOutput, calls=%fused_computation.17 | convolution fusion | flops 2956984320 | bytes 15090688 | tf_op jit(solution)/shard_map/dot_general | solution.py:42
  263.0 68.7 %all-to-all-done = bf16[32,128,1408]{2,1,0:T(8,128)(2,1)} async-done(((bf16[32,128,1408]{2,1,0:T(8,128)(2,1)}), bf16[32,128,1408]{2,1,0:T(8,128)(2,1)}, u32[]{:S(2)}, u32[]{:S(2)}) %all-to-all-start) | async-done | bytes 11534368 | tf_op jit(solution)/shard_map/all_to_all | solution.py:47
  331.7 0.0 copy-start.6
  331.7 9.0 %multiply_reduce_fusion = (f32[256]{0:T(256)S(1)}, bf16[256,1408]{1,0:T(8,128)(2,1)S(1)}) fusion(f32[256,1408]{1,0:T(8,128)} %fusion.11, bf16[256,4096]{1,0:T(8,128)(2,1)} %fusion.1, bf16[4096,1408]{1,0:T(8,128)(2,1)} %bitcast), kind=kOutput, calls=%fused_computation.20 | convolution fusion | flops 2957115136 | bytes 15795200 | tf_op jit(solution)/shard_map/dot_general | solution.py:83
  340.7 0.0 copy-done.6
  340.7 5.0 fusion.23
  345.8 0.0 all-reduce.4.cloned.1.call-update
  345.8 0.2 reduce-scatter.2.cloned.1.call-start
  346.0 9.5 %convolution_convert_fusion = bf16[256,4096]{1,0:T(8,128)(2,1)} fusion(bf16[4096,1408]{1,0:T(8,128)(2,1)} %bitcast, f32[256,1408]{1,0:T(8,128)} %fusion.11), kind=kOutput, calls=%fused_computation.6 | convolution fusion | flops 2955640832 | bytes 15073280 | tf_op jit(solution)/shard_map/dot_general | solution.py:55
  355.5 0.0 reduce-scatter.2.cloned.1.call-update
  355.6 0.0 all-reduce.6.cloned.1.call-start
  355.6 1.8 convolution_multiply_fusion.1
  357.4 0.8 convolution_multiply_fusion.2
  358.2 0.0 all-reduce.6.cloned.1.call-update
  358.3 1.7 constant_dynamic-slice_fusion
  359.9 1.7 multiply_convert_fusion.2
  361.6 22.3 %psum.29 = f32[256]{0:T(256)S(1)} all-reduce(f32[256]{0:T(256)S(1)} %get-tuple-element.10), channel_id=1, replica_groups=mesh['dp'=32,'mp'=8] {'mp'}, use_global_device_ids=true, to_apply=%region_4.5 | all-reduce | flops 256 | bytes 2048 | tf_op jit(solution)/shard_map/psum | solution.py:89
  383.9 80.6 %all-reduce.4.cloned.1.call-done = f32[256,4096]{1,0:T(8,128)} async-done(((f32[256,4096]{1,0:T(8,128)}), f32[256,4096]{1,0:T(8,128)}) %all-reduce.4.cloned.1.call-update) | async-done | bytes 4194320 | tf_op jit(solution)/shard_map/psum | solution.py:89
  464.5 5.8 fusion.8
  470.3 77.5 %reduce-scatter.2.cloned.1.call-done = bf16[256,512]{1,0:T(8,128)(2,1)} async-done(((bf16[256,4096]{1,0:T(8,128)(2,1)}), bf16[256,512]{1,0:T(8,128)(2,1)}) %reduce-scatter.2.cloned.1.call-update) | async-done | bytes 262160 | tf_op jit(solution)/shard_map/reduce_scatter | solution.py:58
  547.9 1.8 multiply_convert_fusion.3
  549.7 228.8 %all-reduce.6.cloned.1.call-done = (f32[512,64]{0,1:T(8,128)}, f32[64,512]{1,0:T(8,128)}) async-done(((f32[512,64]{0,1:T(8,128)}, f32[64,512]{1,0:T(8,128)}), (f32[512,64]{0,1:T(8,128)}, f32[64,512]{1,0:T(8,128)})) %all-reduce.6.cloned.1.call-update) | async-done | bytes 262160 | tf_op jit(solution)/shard_map/psum | solution.py:82
  778.5 1.6 copy.18
  780.1 1.6 copy.19
  (2 shorter events, 0.0 us)
Async XLA Ops:
  7.2 19.7 %copy-start = (bf16[64,4096]{1,0:T(8,128)(2,1)S(1)}, bf16[64,4096]{1,0:T(8,128)(2,1)}, u32[]{:S(2)}) copy-start(bf16[64,4096]{1,0:T(8,128)(2,1)} %param.17) | copy-start | bytes 1572868
  7.2 246.2 %all-gather.2.cloned.1.call-start = ((), (), s32[]{:S(2)}) async-start(), calls=%async_computation.2 | async-start | bytes 11894784 | tf_op jit(solution)/shard_map/all_gather | solution.py:33
  14.5 11.5 %copy-start.5 = (bf16[4096]{0:T(1024)(128)(2,1)S(1)}, bf16[4096]{0:T(1024)(128)(2,1)}, u32[]{:S(2)}) copy-start(bf16[4096]{0:T(1024)(128)(2,1)} %param.13) | copy-start | bytes 24580
  14.5 11.5 %copy-start.2 = (bf16[256,4096]{1,0:T(8,128)(2,1)S(1)}, bf16[256,4096]{1,0:T(8,128)(2,1)}, u32[]{:S(2)}) copy-start(bf16[256,4096]{1,0:T(8,128)(2,1)} %param.9) | copy-start | bytes 6291460
  14.5 11.5 %copy-start.4 = (bf16[4096,64]{0,1:T(8,128)(2,1)S(1)}, bf16[4096,64]{0,1:T(8,128)(2,1)}, u32[]{:S(2)}) copy-start(bf16[4096,64]{0,1:T(8,128)(2,1)} %param.16) | copy-start | bytes 1572868
  14.5 317.2 %all-to-all-start = ((bf16[32,128,1408]{2,1,0:T(8,128)(2,1)}), bf16[32,128,1408]{2,1,0:T(8,128)(2,1)}, u32[]{:S(2)}, u32[]{:S(2)}) async-start(bf16[32,128,1408]{2,1,0:T(8,128)(2,1)} %stack.2), calls=%async_computation | async-start | bytes 23068672 | tf_op jit(solution)/shard_map/all_to_all | solution.py:47
  26.0 438.6 %all-reduce.4.cloned.1.call-start = ((), (), s32[]{:S(2)}) async-start(), calls=%async_computation.4 | async-start | bytes 8388608 | tf_op jit(solution)/shard_map/psum | solution.py:89
  26.0 1.6 copy-start.7
  27.6 2.2 copy-start.1
  29.8 1.7 copy-start.3
  331.7 9.0 %copy-start.6 = (bf16[4096,1408]{1,0:T(8,128)(2,1)S(1)}, bf16[4096,1408]{1,0:T(8,128)(2,1)}, u32[]{:S(2)}) copy-start(bf16[4096,1408]{1,0:T(8,128)(2,1)} %all-gather.2.cloned.1.call-done) | copy-start | bytes 34603012
  345.8 202.1 %reduce-scatter.2.cloned.1.call-start = ((), (), s32[]{:S(2)}) async-start(), calls=%async_computation.3 | async-start | bytes 2359296 | tf_op jit(solution)/shard_map/reduce_scatter | solution.py:58
  355.6 423.0 %all-reduce.6.cloned.1.call-start = ((), (), s32[]{:S(2)}) async-start(), calls=%async_computation.5 | async-start | bytes 524288 | tf_op jit(solution)/shard_map/psum | solution.py:82
Sparse Core Ops, SparseCore 0:
  9.8 243.5 all-gather.1
  345.9 118.5 all-reduce.3
  468.6 79.2 reduce-scatter.1
  551.0 227.5 all-reduce.5
